TPU v7x, 32 devices: a whole 2x2x4 slice. The times are simulated.
32 devices in a mesh: groups: 2 (over x), seq: 16 (over z, y, core).
Axes of the slice: x: 2, y: 2, z: 4, core: 2. Of those that a mesh axis runs over, the one named last changes fastest.
Arguments:
- queries: bfloat16 [16384, 2048], P(('groups', 'seq')), parts along dimension 0, may hold values from -10 to 10
- keys: bfloat16 [16384, 2048], P(('groups', 'seq')), parts along dimension 0, may hold values from -10 to 10
- values: bfloat16 [16384, 2048], P(('groups', 'seq')), parts along dimension 0, may hold values from -6 to 6
- ssd_input: bfloat16 [16384, 2048], P(('groups', 'seq')), parts along dimension 0, may hold values from -6 to 6
- bmat: bfloat16 [16384, 128], P(('groups', 'seq')), parts along dimension 0, may hold values from -0.5 to 0.5
- cmat: bfloat16 [16384, 128], P(('groups', 'seq')), parts along dimension 0, may hold values from -6 to 6
- expo: int32 [16384, 32], P(('groups', 'seq')), parts along dimension 0, may hold values from 1 to 16384
- rate: float32 [32], replicated, may hold values from 1.2207031e-05 to 0.06
- skip: float32 [32], replicated, may hold values from 0.5 to 1.5
Outputs:
- attn_out: bfloat16 [16384, 2048], P(('groups', 'seq')), parts along dimension 0
- normed_recurrence_output: bfloat16 [16384, 2048], P(('groups', 'seq')), parts along dimension 0
There are 2 independent parts, one for each index of `groups`. A program takes and returns all parts, laid end to end along the dimension named above; an argument that names none is the same for every part. Nothing has to cross between parts.
All inputs are finite; a program needn't handle non-finite values.
Results may differ from a plain program's by a relative error of at most 0.0049.
Values may be sent and summed in bfloat16 or wider, within the bound.
A program may use at most 192 MiB of HBM per device.

v0:
```python
import math

import jax
import jax.numpy as jnp
from jax import lax
from jax.sharding import PartitionSpec as P

E = 128
W = 2048
Q = 256


def passed_along(block, axis, distance):
    devices = range(lax.axis_size(axis))
    route = [(i - distance, i) for i in devices if i - distance in devices]
    return lax.ppermute(block, axis, route)


def entering_2(shard, axis, combine, identity):
    peers, here = (lax.axis_size(axis), lax.axis_index(axis))
    everything = jax.tree.map(lambda part: lax.all_gather(part, axis), shard)
    start = jax.tree.map(
        lambda part, zero: jnp.broadcast_to(jnp.asarray(zero, part.dtype), part.shape),
        shard,
        identity,
    )

    def hop(k, before):
        reached = k < here
        new = combine(before, jax.tree.map(lambda part: part[k], everything))
        return jax.tree.map(lambda a, b: jnp.where(reached, a, b), new, before)

    return lax.fori_loop(0, peers, hop, start)


def block_local(piece_x, piece_b, piece_c, piece_loga):
    cumulative = jnp.cumsum(piece_loga, axis=0).T
    block_len = cumulative.shape[1]
    lower_mask = jnp.arange(block_len)[:, None] >= jnp.arange(block_len)[None, :]
    log_gaps = cumulative[:, :, None] - cumulative[:, None, :]
    decay_grid = jnp.where(
        lower_mask[None], jnp.exp(jnp.where(lower_mask[None], log_gaps, 0.0)), 0.0
    )
    cross_term = jnp.dot(piece_c, piece_b.T, preferred_element_type=jnp.float32)
    inner_term = (cross_term[None] * decay_grid).astype(jnp.bfloat16)
    intra_term = jnp.einsum("hts,shp->thp", inner_term, piece_x, preferred_element_type=jnp.float32)
    end_weights = jnp.exp(cumulative[:, -1:] - cumulative)
    weighted = (end_weights.T[:, :, None] * piece_b.astype(jnp.float32)[:, None, :]).astype(
        jnp.bfloat16
    )
    local_state = jnp.einsum("shp,shn->hpn", piece_x, weighted, preferred_element_type=jnp.float32)
    end_decay = jnp.exp(cumulative[:, -1])
    return (intra_term, cumulative, end_decay, local_state)


def block_output(intra_term, cumulative, piece_x, piece_c, skip, carried):
    inter_term = jnp.einsum(
        "tn,hpn->thp",
        piece_c.astype(jnp.float32),
        carried,
        precision=lax.Precision.HIGHEST,
        preferred_element_type=jnp.float32,
    )
    mixed = (
        intra_term
        + inter_term * jnp.exp(cumulative.T)[:, :, None]
        + skip[None, :, None] * piece_x.astype(jnp.float32)
    )
    inv_rms = lax.rsqrt(jnp.mean(mixed * mixed, axis=2, keepdims=True) + 1e-05)
    return (
        (mixed * inv_rms)
        .astype(jnp.bfloat16)
        .reshape(mixed.shape[0], mixed.shape[1] * mixed.shape[2])
    )


def window_attention(queries, keys_all, values_all, first_pos):
    length = queries.shape[0]
    row_width = queries.shape[1]
    head_count = row_width // E
    group_size = math.gcd(head_count, 4)
    group_cols = group_size * E
    block_rows = min(length, 512)
    query_pos = first_pos + 0 + jnp.arange(block_rows, dtype=jnp.int32)
    key_pos = first_pos - W + 0 + jnp.arange(block_rows + W, dtype=jnp.int32)
    visible = (
        (key_pos[None, :] <= query_pos[:, None])
        & (key_pos[None, :] > query_pos[:, None] - W)
        & (key_pos[None, :] >= 0)
    )

    def one_group(group_index, result):
        column = group_index * group_cols
        query_group = lax.dynamic_slice_in_dim(queries, column, group_cols, 1).reshape(
            block_rows, group_size, E
        )
        key_group = lax.dynamic_slice_in_dim(keys_all, column, group_cols, 1).reshape(
            block_rows + W, group_size, E
        )
        value_group = lax.dynamic_slice_in_dim(values_all, column, group_cols, 1).reshape(
            block_rows + W, group_size, E
        )
        scores = jnp.einsum(
            "rge,kge->grk", query_group, key_group, preferred_element_type=jnp.float32
        ) / math.sqrt(E)
        scores = jnp.where(visible[None], scores, -1e30)
        row_max = jnp.max(scores, axis=2, keepdims=True)
        exp_scores = jnp.exp(scores - row_max)
        attn_probs = (exp_scores / jnp.sum(exp_scores, axis=2, keepdims=True)).astype(jnp.bfloat16)
        group_out = jnp.einsum(
            "grk,kge->rge", attn_probs, value_group, preferred_element_type=jnp.float32
        )
        group_out = group_out.reshape(block_rows, group_cols).astype(jnp.bfloat16)
        return lax.dynamic_update_slice_in_dim(result, group_out, column, 1)

    results = lax.fori_loop(
        0, head_count // group_size, one_group, jnp.zeros((block_rows, row_width), jnp.bfloat16)
    )
    return results


def on_device(queries, keys, values, ssd_input, bmat, cmat, expo, rate, skip):
    length = queries.shape[0]
    first_pos = lax.axis_index("seq") * length
    kv_pair = jnp.stack([keys, values])
    span_shards = W // length
    relayed = kv_pair
    earlier = []
    for distance in range(span_shards):
        relayed = passed_along(relayed, "seq", 1)
        earlier.insert(0, relayed)
    joined = jnp.concatenate(earlier + [kv_pair], axis=1)
    attn_out = window_attention(queries, joined[0], joined[1], first_pos)
    head_count = rate.shape[0]
    head_dim = ssd_input.shape[1] // head_count
    state_size = cmat.shape[1]
    block_count = length // Q
    all_x = ssd_input.reshape(length, head_count, head_dim)
    all_loga = -rate[None, :] * expo.astype(jnp.float32)
    locals_list = []
    dev_decay = jnp.ones((head_count,), jnp.float32)
    dev_state = jnp.zeros((head_count, head_dim, state_size), jnp.float32)
    for block_index in range(block_count):
        lower = block_index * Q
        parts_now = block_local(
            all_x[lower : lower + Q],
            bmat[lower : lower + Q],
            cmat[lower : lower + Q],
            all_loga[lower : lower + Q],
        )
        locals_list.append(parts_now)
        dev_state = parts_now[2][:, None, None] * dev_state + parts_now[3]
        dev_decay = dev_decay * parts_now[2]

    def link(earlier_pair, later_pair):
        return (
            earlier_pair[0] * later_pair[0],
            later_pair[0][:, None, None] * earlier_pair[1] + later_pair[1],
        )

    identity = (
        jnp.ones((head_count,), jnp.float32),
        jnp.zeros((head_count, head_dim, state_size), jnp.float32),
    )
    entering = entering_2((dev_decay, dev_state), "seq", link, identity)
    carried = entering[1]
    outputs = []
    for block_index in range(block_count):
        lower = block_index * Q
        intra_term, cumulative, end_decay, local_state = locals_list[block_index]
        outputs.append(
            block_output(
                intra_term,
                cumulative,
                all_x[lower : lower + Q],
                cmat[lower : lower + Q],
                skip,
                carried,
            )
        )
        carried = end_decay[:, None, None] * carried + local_state
    normed_recurrence_output = jnp.concatenate(outputs, axis=0)
    return (attn_out, normed_recurrence_output)


def solution(mesh):
    placed = (
        P(("groups", "seq"), None),
        P(("groups", "seq"), None),
        P(("groups", "seq"), None),
        P(("groups", "seq"), None),
        P(("groups", "seq"), None),
        P(("groups", "seq"), None),
        P(("groups", "seq"), None),
        P(),
        P(),
    )
    return jax.shard_map(
        on_device,
        mesh=mesh,
        in_specs=placed,
        out_specs=(P(("groups", "seq"), None), P(("groups", "seq"), None)),
        check_vma=False,
    )
```

profile of v0, /device:TPU:8, one launch (start us, length us, event | category | flops | bytes accessed | tf_op | source)
XLA Modules:
  0.0 584.1 jit_solution(17286876546489918469)
XLA Ops:
  11.8 48.8 %collective-permute-done = bf16[2,512,2048]{2,1,0:T(8,128)(2,1)S(1)} collective-permute-done((bf16[2,512,2048]{2,1,0:T(8,128)(2,1)S(1)}, bf16[2,512,2048]{2,1,0:T(8,128)(2,1)S(1)}, u32[]{:S(2)}, u32[]{:S(2)}) %collective-permute-start) | collective-permute-done | bytes 4194336 | tf_op jit(solution)/shard_map/ppermute | solution.py:16
  64.4 48.9 %collective-permute-done.1 = bf16[2,512,2048]{2,1,0:T(8,128)(2,1)} collective-permute-done((bf16[2,512,2048]{2,1,0:T(8,128)(2,1)S(1)}, bf16[2,512,2048]{2,1,0:T(8,128)(2,1)}, u32[]{:S(2)}, u32[]{:S(2)}) %collective-permute-start.1) | collective-permute-done | bytes 4194336 | tf_op jit(solution)/shard_map/ppermute | solution.py:16
  124.1 40.3 %collective-permute-done.2 = bf16[2,512,2048]{2,1,0:T(8,128)(2,1)} collective-permute-done((bf16[2,512,2048]{2,1,0:T(8,128)(2,1)}, bf16[2,512,2048]{2,1,0:T(8,128)(2,1)}, u32[]{:S(2)}, u32[]{:S(2)}) %collective-permute-start.2) | collective-permute-done | bytes 4194336 | tf_op jit(solution)/shard_map/ppermute | solution.py:16
  170.4 137.7 %all-reduce = f32[512]{0:T(512)S(1)} all-reduce(f32[512]{0:T(512)S(1)} %dynamic-update-slice), channel_id=2, replica_groups=mesh['groups'=2,'seq'=16] {'seq'}, use_global_device_ids=true, to_apply=%add | all-reduce | flops 512 | bytes 4096
  322.5 7.4 %slice_bitcast_fusion = (bf16[2560,2048]{1,0:T(8,128)(2,1)}, bf16[2560,2048]{1,0:T(8,128)(2,1)}) fusion(bf16[2,2560,2048]{2,1,0:T(8,128)(2,1)S(1)} %constant_dynamic-update-slice_fusion.1), kind=kLoop, calls=%fused_computation.22 | loop fusion | bytes 41943040 | tf_op jit(solution)/shard_map/squeeze | solution.py:133
  331.4 174.4 %while.28 = (s32[]{:T(128)}, bf16[512,2048]{1,0:T(8,128)(2,1)}, bf16[2560,2048]{1,0:T(8,128)(2,1)}, bf16[512,2048]{1,0:T(8,128)(2,1)}, bf16[2560,2048]{1,0:T(8,1...) while((s32[]{:T(128)}, bf16[512,2048]{1,0:T(8,128)(2,1)}, ...), condition=%wide.region_3.4_spmd.clone, body=%wide.region_0.3_spmd.clone.sunk | while | flops 2721319424 | bytes 76055216 | solution.py:116
  331.4 4.4 constant_dynamic-slice_fusion.5
  335.8 4.4 copy.97
  346.0 13.8 %fusion.78 = (f32[4,512]{1,0:T(4,128)S(1)}, f32[4,512,2560]{2,1,0:T(8,128)}) fusion(pred[512,2560]{1,0:T(8,128)(4,1)} %and_and_fusion.2, bf16[512,4,128]{0,2,1:T(8,128)(2,1)} %bitcast.120, bf16[2560,4,128]{0,2,1:T(8,128)(2,1)} %bitcast.118), kind=kOutput, calls=%fused_computation.111.clone.1 | convolution fusion | flops 1363151360 | bytes 25436160 | tf_op jit(solution)/shard_map/while/body/eval_jaxpr/sub | solution.py:108
  362.6 11.4 %fusion.79 = bf16[4,128,512]{2,1,0:T(8,128)(2,1)S(1)} fusion(bf16[2560,4,128]{0,2,1:T(8,128)(2,1)} %bitcast.119, f32[4,512,2560]{2,1,0:T(8,128)} %get-tuple-element.428, f32[4,512]{1,0:T(4,128)S(1)} %get-tuple-element.429), kind=kOutput, calls=%fused_computation.12.clone.1 | convolution fusion | flops 1352925184 | bytes 24125440 | tf_op jit(solution)/shard_map/while/body/eval_jaxpr/grk,kge->rge/dot_general | solution.py:110
  375.0 4.4 constant_dynamic-slice_fusion.5
  379.4 4.4 copy.97
  389.6 13.8 %fusion.78 = (f32[4,512]{1,0:T(4,128)S(1)}, f32[4,512,2560]{2,1,0:T(8,128)}) fusion(pred[512,2560]{1,0:T(8,128)(4,1)} %and_and_fusion.2, bf16[512,4,128]{0,2,1:T(8,128)(2,1)} %bitcast.120, bf16[2560,4,128]{0,2,1:T(8,128)(2,1)} %bitcast.118), kind=kOutput, calls=%fused_computation.111.clone.1 | convolution fusion | flops 1363151360 | bytes 25436160 | tf_op jit(solution)/shard_map/while/body/eval_jaxpr/sub | solution.py:108
  406.2 11.4 %fusion.79 = bf16[4,128,512]{2,1,0:T(8,128)(2,1)S(1)} fusion(bf16[2560,4,128]{0,2,1:T(8,128)(2,1)} %bitcast.119, f32[4,512,2560]{2,1,0:T(8,128)} %get-tuple-element.428, f32[4,512]{1,0:T(4,128)S(1)} %get-tuple-element.429), kind=kOutput, calls=%fused_computation.12.clone.1 | convolution fusion | flops 1352925184 | bytes 24125440 | tf_op jit(solution)/shard_map/while/body/eval_jaxpr/grk,kge->rge/dot_general | solution.py:110
  418.6 4.4 constant_dynamic-slice_fusion.5
  423.0 4.4 copy.97
  433.2 13.8 %fusion.78 = (f32[4,512]{1,0:T(4,128)S(1)}, f32[4,512,2560]{2,1,0:T(8,128)}) fusion(pred[512,2560]{1,0:T(8,128)(4,1)} %and_and_fusion.2, bf16[512,4,128]{0,2,1:T(8,128)(2,1)} %bitcast.120, bf16[2560,4,128]{0,2,1:T(8,128)(2,1)} %bitcast.118), kind=kOutput, calls=%fused_computation.111.clone.1 | convolution fusion | flops 1363151360 | bytes 25436160 | tf_op jit(solution)/shard_map/while/body/eval_jaxpr/sub | solution.py:108
  449.8 11.4 %fusion.79 = bf16[4,128,512]{2,1,0:T(8,128)(2,1)S(1)} fusion(bf16[2560,4,128]{0,2,1:T(8,128)(2,1)} %bitcast.119, f32[4,512,2560]{2,1,0:T(8,128)} %get-tuple-element.428, f32[4,512]{1,0:T(4,128)S(1)} %get-tuple-element.429), kind=kOutput, calls=%fused_computation.12.clone.1 | convolution fusion | flops 1352925184 | bytes 24125440 | tf_op jit(solution)/shard_map/while/body/eval_jaxpr/grk,kge->rge/dot_general | solution.py:110
  462.2 4.4 constant_dynamic-slice_fusion.5
  466.6 4.4 copy.97
  476.8 13.8 %fusion.78 = (f32[4,512]{1,0:T(4,128)S(1)}, f32[4,512,2560]{2,1,0:T(8,128)}) fusion(pred[512,2560]{1,0:T(8,128)(4,1)} %and_and_fusion.2, bf16[512,4,128]{0,2,1:T(8,128)(2,1)} %bitcast.120, bf16[2560,4,128]{0,2,1:T(8,128)(2,1)} %bitcast.118), kind=kOutput, calls=%fused_computation.111.clone.1 | convolution fusion | flops 1363151360 | bytes 25436160 | tf_op jit(solution)/shard_map/while/body/eval_jaxpr/sub | solution.py:108
  493.4 11.4 %fusion.79 = bf16[4,128,512]{2,1,0:T(8,128)(2,1)S(1)} fusion(bf16[2560,4,128]{0,2,1:T(8,128)(2,1)} %bitcast.119, f32[4,512,2560]{2,1,0:T(8,128)} %get-tuple-element.428, f32[4,512]{1,0:T(4,128)S(1)} %get-tuple-element.429), kind=kOutput, calls=%fused_computation.12.clone.1 | convolution fusion | flops 1352925184 | bytes 24125440 | tf_op jit(solution)/shard_map/while/body/eval_jaxpr/grk,kge->rge/dot_general | solution.py:110
  505.9 54.3 %while.29 = (s32[]{:T(128)}, f32[32,64,128]{2,1,0:T(8,128)}, s32[]{:T(128)}, f32[16,32]{1,0:T(8,128)}, f32[16,32,64,128]{3,2,1,0:T(8,128)}, /*index=5*/s32[]{:T(128)}, s32[]{:T(128)}) while((s32[]{:T(128)}, f32[32,64,128]{2,1,0:T(8,128)}, s32[]{:T(128)}, f32[16,32]{1,0:T(8,128)}, f32[16,32,64,128]{3,2,1,0:T(8,128)}, ...), condition=%wide.region_9.10_spmd.clone, body=%wide.region_8.9_spmd.clone.sunk | while | flops 1048580 | bytes 3146217 | solution.py:33
  570.2 4.6 multiply_reduce_fusion.1
  (171 shorter events, 145.0 us)
Async XLA Ops:
  7.2 498.7 %all-gather.4.cloned.1.call-start = ((), (), s32[]{:S(2)}) async-start(), calls=%async_computation | async-start | bytes 17825792 | tf_op jit(solution)/shard_map/all_gather | solution.py:21
  7.2 108.1 %copy-start.24 = (f32[32]{0:T(128)S(1)}, f32[32]{0:T(128)}, u32[]{:S(2)}) copy-start(f32[32]{0:T(128)} %param.20) | copy-start | bytes 388
  7.2 108.1 %copy-start.19 = (s32[512,32]{0,1:T(8,128)S(1)}, s32[512,32]{0,1:T(8,128)}, u32[]{:S(2)}) copy-start(s32[512,32]{0,1:T(8,128)} %param.19) | copy-start | bytes 196612
  9.9 50.7 %collective-permute-start = (bf16[2,512,2048]{2,1,0:T(8,128)(2,1)S(1)}, bf16[2,512,2048]{2,1,0:T(8,128)(2,1)S(1)}, u32[]{:S(2)}, u32[]{:S(2)}) collective-permute-start(bf16[2,512,2048]{2,1,0:T(8,128)(2,1)S(1)} %pad_maximum_fusion), channel_id=1, source_target_pairs={{0,1},{1,2},{2,3},{3,4},{4,5},{5,6},{6,7},{7,8},{8,9},{9,10},{10,1... | collective-permute-start | bytes 12582920 | tf_op jit(solution)/shard_map/ppermute | solution.py:16
  62.5 50.8 %collective-permute-start.1 = (bf16[2,512,2048]{2,1,0:T(8,128)(2,1)S(1)}, bf16[2,512,2048]{2,1,0:T(8,128)(2,1)}, u32[]{:S(2)}, u32[]{:S(2)}) collective-permute-start(bf16[2,512,2048]{2,1,0:T(8,128)(2,1)S(1)} %collective-permute-done), channel_id=1, source_target_pairs={{0,1},{1,2},{2,3},{3,4},{4,5},{5,6},{6,7},{7,8},{8,9},{9,10},{10,1... | collective-permute-start | bytes 12582920 | tf_op jit(solution)/shard_map/ppermute | solution.py:16
  113.3 51.0 %collective-permute-start.2 = (bf16[2,512,2048]{2,1,0:T(8,128)(2,1)}, bf16[2,512,2048]{2,1,0:T(8,128)(2,1)}, u32[]{:S(2)}, u32[]{:S(2)}) collective-permute-start(bf16[2,512,2048]{2,1,0:T(8,128)(2,1)} %collective-permute-done.1), channel_id=1, source_target_pairs={{0,1},{1,2},{2,3},{3,4},{4,5},{5,6},{6,7},{7,8},{8,9},{9,10},{10,1... | collective-permute-start | bytes 12582920 | tf_op jit(solution)/shard_map/ppermute | solution.py:16
  117.0 5.6 copy-start.12
  119.2 49.6 %copy-start.6 = (bf16[256,2048]{0,1:T(8,128)(2,1)}, bf16[256,2048]{0,1:T(8,128)(2,1)S(1)}, u32[]{:S(2)}) copy-start(bf16[256,2048]{0,1:T(8,128)(2,1)S(1)} %copy.61) | copy-start | bytes 3145732
  120.7 190.5 %copy-start.8 = (bf16[256,2048]{0,1:T(8,128)(2,1)}, bf16[256,2048]{0,1:T(8,128)(2,1)S(1)}, u32[]{:S(2)}) copy-start(bf16[256,2048]{0,1:T(8,128)(2,1)S(1)} %copy.64) | copy-start | bytes 3145732
  120.7 48.2 %copy-start.26 = (u32[32]{0:T(128)S(1)}, u32[32]{0:T(128)}, u32[]{:S(2)}) copy-start(u32[32]{0:T(128)} %constant.106) | copy-start | bytes 388
  120.7 188.7 %copy-start.10 = (bf16[512,128]{1,0:T(8,128)(2,1)S(1)}, bf16[512,128]{1,0:T(8,128)(2,1)}, u32[]{:S(2)}) copy-start(bf16[512,128]{1,0:T(8,128)(2,1)} %param.18) | copy-start | bytes 393220
  124.1 42.2 %copy-start.4 = (f32[32,64,128]{2,1,0:T(8,128)}, f32[32,64,128]{2,1,0:T(8,128)S(1)}, u32[]{:S(2)}) copy-start(f32[32,64,128]{2,1,0:T(8,128)S(1)} %fusion.38) | copy-start | bytes 3145732
  164.4 146.8 %collective-permute-start.3 = (bf16[2,512,2048]{2,1,0:T(8,128)(2,1)}, bf16[2,512,2048]{2,1,0:T(8,128)(2,1)}, u32[]{:S(2)}, u32[]{:S(2)}) collective-permute-start(bf16[2,512,2048]{2,1,0:T(8,128)(2,1)} %collective-permute-done.2), channel_id=1, source_target_pairs={{0,1},{1,2},{2,3},{3,4},{4,5},{5,6},{6,7},{7,8},{8,9},{9,10},{10,1... | collective-permute-start | bytes 12582920 | tf_op jit(solution)/shard_map/ppermute | solution.py:16
  316.2 3.5 copy-start.3
  319.7 2.2 copy-start.1
  505.9 54.4 %copy-start.11 = (bf16[512,128]{1,0:T(8,128)(2,1)S(1)}, bf16[512,128]{1,0:T(8,128)(2,1)}, u32[]{:S(2)}) copy-start(bf16[512,128]{1,0:T(8,128)(2,1)} %param.18) | copy-start | bytes 393220
  505.9 58.0 %copy-start.5 = (f32[32,64,128]{2,1,0:T(8,128)S(1)}, f32[32,64,128]{2,1,0:T(8,128)}, u32[]{:S(2)}) copy-start(f32[32,64,128]{2,1,0:T(8,128)} %copy-done.4) | copy-start | bytes 3145732
  505.9 58.0 %copy-start.23 = (f32[32]{0:T(128)S(1)}, f32[32]{0:T(128)}, u32[]{:S(2)}) copy-start(f32[32]{0:T(128)} %get-tuple-element.331) | copy-start | bytes 388
  560.2 6.0 %copy-start.9 = (bf16[256,2048]{0,1:T(8,128)(2,1)S(1)}, bf16[256,2048]{0,1:T(8,128)(2,1)}, u32[]{:S(2)}) copy-start(bf16[256,2048]{0,1:T(8,128)(2,1)} %copy-done.8) | copy-start | bytes 3145732
  560.2 6.0 %copy-start.14 = (f32[256,256]{1,0:T(8,128)S(1)}, f32[256,256]{1,0:T(8,128)}, u32[]{:S(2)}) copy-start(f32[256,256]{1,0:T(8,128)} %fusion.47) | copy-start | bytes 786436
  560.2 6.0 %copy-start.18 = (f32[32,256]{1,0:T(8,128)S(1)}, f32[32,256]{1,0:T(8,128)}, u32[]{:S(2)}) copy-start(f32[32,256]{1,0:T(8,128)} %copy-done.17) | copy-start | bytes 98308
  560.2 6.0 %copy-start.20 = (pred[256,256]{1,0:T(8,128)(4,1)S(1)}, pred[256,256]{1,0:T(8,128)(4,1)}, u32[]{:S(2)}) copy-start(pred[256,256]{1,0:T(8,128)(4,1)} %iota_compare_fusion) | copy-start | bytes 196612
  560.2 6.0 %copy-start.22 = (f32[256,32]{0,1:T(8,128)S(1)}, f32[256,32]{0,1:T(8,128)}, u32[]{:S(2)}) copy-start(f32[256,32]{0,1:T(8,128)} %get-tuple-element.329) | copy-start | bytes 98308
  560.2 6.0 %copy-start.25 = (f32[32]{0:T(128)S(1)}, f32[32]{0:T(128)}, u32[]{:S(2)}) copy-start(f32[32]{0:T(128)} %param.21) | copy-start | bytes 388
  (8 other events, 10.0 us)
Sparse Core Ops, SparseCore 0:
  169.0 152.1 all-gather.3
where the time goes:
time: 591 us; the launch traced here: 584 us
  waiting for transfers between devices  138 us (23%)
  blocking collectives  138 us (23%)
  matrix products  120 us (20%)
  local copies, waits for them, and re-layouts  98.3 us (17%)
  other arithmetic  67.1 us (11%)
  between operations  15.1 us (3%)
  starting transfers between devices  7.69 us (1%)
    ppermute x4, waiting for transfers between devices, passed_along(): return lax.ppermute(block, axis, route)  138 us
    unnamed x1, blocking collectives  138 us
    sub x4, matrix products, one_group(): exp_scores = jnp.exp(scores - row_max)  55.1 us
    dot_general x4, matrix products, one_group(): jnp.einsum('grk,kge->rge', attn_probs, value_group, preferred_element_typ...  45.7 us
    select_n x16, other arithmetic, hop(): return jax.tree.map(lambda a, b: jnp.where(reached, a, b), new, before)  43 us
    dynamic_slice x8, local copies, waits for them, and re-layouts, one_group(): lax.dynamic_slice_in_dim(keys_all, column, group_cols, 1)  35.2 us
    and x4, other arithmetic, window_attention(): (key_pos[None, :] <= query_pos[:, None]) & (key_pos[None, :] > query_pos[...  14.6 us
    unnamed x62, local copies, waits for them, and re-layouts  14.3 us
  transfers between devices with their start and end apart: 5, of which 3 were waited for; matrix products, arithmetic and copies ran while one was open for 35% of the time, Pallas kernels for 0%

commit v1 on v0

v1 whole, which is shorter than its diff:
```python
import functools
import math

import jax
import jax.numpy as jnp
from jax import lax
from jax.experimental import pallas as pl
from jax.experimental.pallas import tpu as pltpu
from jax.sharding import PartitionSpec as P

E = 128
W = 2048
Q = 256
CHUNK = 256
AHEAD = 3
NEG = -1e30
LOG2E = math.log2(math.e)
MESH = pl.DeviceIdType.MESH
Z, Y, A, B = range(4)


def dot(a, b):
    return jnp.dot(a, b, preferred_element_type=jnp.float32)


def dot_t(a, b):
    return lax.dot_general(a, b, (((1,), (1,)), ((), ())), preferred_element_type=jnp.float32)


def attend(bias, q_ref, ko_ref, vo_ref, held, out_ref, chunk):
    length = q_ref.shape[0]
    tq = min(256, length)
    scale = LOG2E / math.sqrt(E)
    row = lax.broadcasted_iota(jnp.int32, (tq, tq), 0)
    col = lax.broadcasted_iota(jnp.int32, (tq, tq), 1)
    for head in range(CHUNK // E):
        wide = pl.ds(pl.multiple_of(chunk * CHUNK + head * E, E), E)
        near = slice(head * E, (head + 1) * E)
        for r in range(0, length, tq):
            q = q_ref[r : r + tq, wide]
            tiles = [(None, r, tq, "low")]
            if r > 0:
                tiles.append((None, 0, r, None))
            tiles.append((Z, r, tq, "up"))
            if r + tq < length:
                tiles.append((Z, r + tq, length - r - tq, None))
            tiles += [(n, 0, length, None) for n in (Y, A, B)]
            m = l = acc = None
            for kind, start, size, mask in tiles:
                rows = slice(start, start + size)
                if kind is None:
                    k, v = ko_ref[rows, wide], vo_ref[rows, wide]
                else:
                    k, v = held[kind, chunk, 0, rows, near], held[kind, chunk, 1, rows, near]
                s = dot_t(q, k) * scale
                if mask == "low":
                    s = jnp.where(col <= row, s, NEG)
                elif mask == "up":
                    s = jnp.where(col > row, s, NEG)
                peak = jnp.max(s, axis=1, keepdims=True)
                if kind is not None:
                    peak = peak + bias[kind]
                m_new = peak if m is None else jnp.maximum(m, peak)
                shift = m_new if kind is None else m_new - bias[kind]
                p = jnp.exp2(s - shift)
                total = jnp.sum(p, axis=1, keepdims=True)
                part = dot(p.astype(jnp.bfloat16), v)
                if m is None:
                    l, acc = total, part
                else:
                    alpha = jnp.exp2(m - m_new)
                    l = l * alpha + total
                    acc = acc * alpha + part
                m = m_new
            out_ref[r : r + tq, wide] = (acc / l).astype(out_ref.dtype)


def pair_columns(lane, table, j, width):
    return jnp.where(lane < width, table[:, 2 * j : 2 * j + 1], table[:, 2 * j + 1 : 2 * j + 2])


def local_states(x_ref, bt_ref, end_ref, decay_ref, local, total):
    rows, total_cols = x_ref.shape
    head_count = end_ref.shape[1]
    width = total_cols // head_count
    lane = lax.broadcasted_iota(jnp.int32, (1, 2 * width), 1)
    weights = jnp.exp(end_ref[...])
    for j in range(head_count // 2):
        cs = slice(2 * width * j, 2 * width * (j + 1))
        state = None
        for block in range(rows // Q):
            rs = slice(block * Q, (block + 1) * Q)
            xs = x_ref[rs, cs].astype(jnp.float32) * pair_columns(lane, weights[rs], j, width)
            one = dot(bt_ref[:, rs], xs.astype(jnp.bfloat16))
            local[block, :, cs] = one
            state = one if state is None else state * decay_ref[block : block + 1, cs] + one
        total[:, cs] = state.astype(jnp.bfloat16)


def recurrence(block, x_ref, b_ref, c_ref, cum_ref, cumt_ref, skip_ref, carried_ref, local, decay_ref, out_ref):
    rows, total_cols = x_ref.shape
    head_count = cum_ref.shape[1]
    width = total_cols // head_count
    pair = 2 * width
    lane = lax.broadcasted_iota(jnp.int32, (1, pair), 1)
    low = lax.broadcasted_iota(jnp.int32, (Q, Q), 1) <= lax.broadcasted_iota(jnp.int32, (Q, Q), 0)
    same = (lax.broadcasted_iota(jnp.int32, (pair, pair), 0) < width) == (
        lax.broadcasted_iota(jnp.int32, (pair, pair), 1) < width
    )
    ones = jnp.where(same, 1.0, 0.0).astype(jnp.bfloat16)
    rs = slice(block * Q, (block + 1) * Q)
    c = c_ref[rs, :]
    cross = jnp.where(low, dot_t(c, b_ref[rs, :]), 0.0)
    cum = cum_ref[rs, :]
    grown = jnp.exp(cum)
    for j in range(head_count // 2):
        cs = slice(pair * j, pair * (j + 1))
        x = x_ref[rs, cs]
        intra = []
        for h in (2 * j, 2 * j + 1):
            gap = cum[:, h : h + 1] - cumt_ref[h : h + 1, rs]
            grid = jnp.exp(jnp.minimum(gap, 0.0))
            intra.append(dot((cross * grid).astype(jnp.bfloat16), x))
        carried = carried_ref[:, cs].astype(jnp.float32)
        for b in range(block):
            carried = carried * decay_ref[b : b + 1, cs] + local[b, :, cs]
        high = carried.astype(jnp.bfloat16)
        inter = dot(c, high)
        if block:
            inter = inter + dot(c, (carried - high.astype(jnp.float32)).astype(jnp.bfloat16))
        mixed = (
            jnp.where(lane < width, intra[0], intra[1])
            + inter * pair_columns(lane, grown, j, width)
            + skip_ref[:, cs] * x.astype(jnp.float32)
        )
        square = mixed * mixed
        big = square.astype(jnp.bfloat16)
        small = (square - big.astype(jnp.float32)).astype(jnp.bfloat16)
        mean = (dot(big, ones) + dot(small, ones)) * (1.0 / width)
        out_ref[rs, cs] = (mixed * lax.rsqrt(mean + 1e-05)).astype(out_ref.dtype)


def kernel(
    size, q_ref, k_ref, v_ref, x_ref, b_ref, bt_ref, c_ref, cum_ref, cumt_ref, end_ref, decay_ref,
    dev_ref, skip_ref, attn_ref, rec_ref, held, local, total, got_s, got_d, sum_q, dec_q, far_s,
    far_d, parts, carried, send, recv, send1, recv1, send2, recv2, send3, recv3,
):
    quads = size // 4
    here = lax.axis_index("seq")
    mine = lax.axis_index("groups")
    quad = here // 4
    member = here % 4
    row = member // 2
    core = member % 2
    chunks = k_ref.shape[1] // CHUNK
    group = total.shape[1] // 4
    blocks = x_ref.shape[0] // Q

    def other(d):
        return 2 * (1 - row if d // 2 else row) + (1 - core if d % 2 else core)

    def beside(d):
        return (mine, quad * 4 + other(d))

    def beyond(e):
        return (mine, (quad + e) % quads * 4 + member)

    def copy(src, dst, sender, receiver, device):
        return pltpu.make_async_remote_copy(
            src_ref=src, dst_ref=dst, send_sem=sender, recv_sem=receiver,
            device_id=device, device_id_type=MESH,
        )

    barrier = pltpu.get_barrier_semaphore()
    for d in range(1, 4):
        pl.semaphore_signal(barrier, inc=1, device_id=beside(d), device_id_type=MESH)
    for e in range(1, quads):
        pl.semaphore_signal(barrier, inc=1, device_id=beyond(e), device_id_type=MESH)
    pl.semaphore_wait(barrier, 3 + quads - 1)

    target = {Z: beyond(1), Y: beside(2), A: beside(1), B: beside(1)}

    def move(kind, chunk, part, src):
        return copy(
            src, held.at[kind, chunk, part], send.at[kind, chunk, part],
            recv.at[kind, chunk, part], target[kind],
        )

    def send_own(kind, chunk):
        wide = pl.ds(pl.multiple_of(chunk * CHUNK, CHUNK), CHUNK)
        for part, ref in ((0, k_ref), (1, v_ref)):
            move(kind, chunk, part, ref.at[:, wide]).start()

    def pass_on(kind, chunk, source):
        for part in range(2):
            move(kind, chunk, part, held.at[source, chunk, part]).start()

    def arrived(kind, chunk):
        for part in range(2):
            move(kind, chunk, part, held.at[kind, chunk, part]).wait_recv()

    def offer(chunk):
        send_own(Z, chunk)

        @pl.when(row == 0)
        def _():
            send_own(Y, chunk)

        @pl.when(core == 0)
        def _():
            send_own(B, chunk)

    def relay(chunk):
        arrived(Z, chunk)

        @pl.when(row == 1)
        def _():
            pass_on(Y, chunk, Z)

        @pl.when(core == 1)
        def _():
            pass_on(B, chunk, Z)

    for chunk in range(min(AHEAD, chunks)):
        offer(chunk)

    def columns(which):
        return pl.ds(pl.multiple_of(which * group, group), group)

    local_states(x_ref, bt_ref, end_ref, decay_ref, local, total)

    def to_member(d):
        at = columns(other(d))
        return (
            copy(total.at[:, at], got_s.at[d], send1.at[0, d], recv1.at[0, d], beside(d)),
            copy(dev_ref.at[:, at], got_d.at[d], send1.at[1, d], recv1.at[1, d], beside(d)),
        )

    def to_quad(e):
        return (
            copy(sum_q, far_s.at[e], send2.at[0, e], recv2.at[0, e], beyond(e)),
            copy(dec_q, far_d.at[e], send2.at[1, e], recv2.at[1, e], beyond(e)),
        )

    def to_owner(d):
        return copy(
            parts.at[other(d)], carried.at[:, columns(member)], send3.at[d], recv3.at[d], beside(d)
        )

    for d in range(1, 4):
        for one in to_member(d):
            one.start()
    got_s[0] = total[:, columns(member)]
    got_d[0] = dev_ref[:, columns(member)]
    for d in range(1, 4):
        for one in to_member(d):
            one.wait_recv()

    def slot(j):
        return jnp.abs(j // 2 - row) * 2 + jnp.abs(j % 2 - core)

    def state_of(j):
        return got_s[slot(j)].astype(jnp.float32)

    def decay_of(j):
        return got_d[slot(j)]

    sums = state_of(0)
    decays = decay_of(0)
    for j in range(1, 4):
        sums = sums * decay_of(j)[0:1] + state_of(j)
        decays = decays * decay_of(j)
    sum_q[...] = sums.astype(jnp.bfloat16)
    dec_q[...] = decays
    for e in range(1, quads):
        for one in to_quad(e):
            one.start()

    def spread():
        for e in range(1, quads):
            for one in to_quad(e):
                one.wait_recv()
        entry = jnp.zeros(sum_q.shape, jnp.float32)
        for e in range(quads - 1, 0, -1):
            grown = entry * far_d[e][0:1] + far_s[e].astype(jnp.float32)
            entry = jnp.where(quad >= e, grown, entry)
        for j in range(4):
            parts[j] = entry.astype(jnp.bfloat16)
            if j < 3:
                entry = entry * decay_of(j)[0:1] + state_of(j)
        for d in range(1, 4):
            to_owner(d).start()
        carried[:, columns(member)] = parts[member]

    def finish(block):
        recurrence(
            block, x_ref, b_ref, c_ref, cum_ref, cumt_ref, skip_ref, carried, local, decay_ref, rec_ref
        )

    def off(seen):
        return jnp.where(seen, 0.0, NEG).astype(jnp.float32)

    inside = quad > 0
    bias = {
        Z: off(inside),
        Y: off(inside | (row == 1)),
        A: off(inside | (row == 1)),
        B: off(inside | (core == 1)),
    }

    relay(0)

    def step(j, carry):
        @pl.when(j + AHEAD < chunks)
        def _():
            offer(j + AHEAD)

        @pl.when(j + 1 < chunks)
        def _():
            relay(j + 1)

        @pl.when(j < chunks)
        def _():
            arrived(Y, j)
            pass_on(A, j, Y)

        @pl.when(j > 0)
        def _():
            arrived(A, j - 1)
            arrived(B, j - 1)
            attend(bias, q_ref, k_ref, v_ref, held, attn_ref, j - 1)

        @pl.when(j == 2)
        def _():
            spread()

        for block in range(blocks):

            @pl.when(j == min(4 + block, chunks))
            def _():
                if block == 0:
                    for d in range(1, 4):
                        copy(
                            parts.at[other(d)], carried.at[:, columns(other(d))], send3.at[d],
                            recv3.at[d], beside(d),
                        ).wait_recv()
                finish(block)

        return carry

    lax.fori_loop(0, chunks + 1, step, 0)

    for d in range(1, 4):
        for one in to_member(d):
            one.wait_send()
        to_owner(d).wait_send()
    for e in range(1, quads):
        for one in to_quad(e):
            one.wait_send()

    def drain(j, carry):
        for kind in range(4):
            for part in range(2):
                move(kind, j, part, held.at[kind, j, part]).wait_send()
        return carry

    lax.fori_loop(0, chunks, drain, 0)


def on_device(queries, keys, values, ssd_input, bmat, cmat, expo, rate, skip):
    length, total_cols = queries.shape
    size = lax.axis_size("seq")
    head_count = rate.shape[0]
    x_cols = ssd_input.shape[1]
    width = x_cols // head_count
    blocks = length // Q
    state = cmat.shape[1]
    group = x_cols // 4
    quads = size // 4
    chunks = total_cols // CHUNK

    loga = -rate[None, :] * expo.astype(jnp.float32)
    cum3 = jnp.cumsum(loga.reshape(blocks, Q, head_count), axis=1)
    ends = cum3[:, -1, :]
    cum = cum3.reshape(length, head_count)
    end_gap = (ends[:, None, :] - cum3).reshape(length, head_count)
    decay_cols = jnp.repeat(jnp.exp(ends), width, axis=1)
    dev = jnp.broadcast_to(jnp.prod(decay_cols, axis=0, keepdims=True), (8, x_cols))
    args = (
        queries, keys, values, ssd_input, bmat, bmat.T, cmat, cum, cum.T, end_gap, decay_cols, dev,
        jnp.repeat(skip, width)[None, :],
    )
    vmem = pl.BlockSpec(memory_space=pltpu.VMEM)
    dma = pltpu.SemaphoreType.DMA
    return pl.pallas_call(
        functools.partial(kernel, size),
        in_specs=[vmem] * len(args),
        out_specs=(vmem, vmem),
        out_shape=(
            jax.ShapeDtypeStruct(queries.shape, jnp.bfloat16),
            jax.ShapeDtypeStruct(ssd_input.shape, jnp.bfloat16),
        ),
        scratch_shapes=[
            pltpu.VMEM((4, chunks, 2, length, CHUNK), jnp.bfloat16),
            pltpu.VMEM((blocks, state, x_cols), jnp.float32),
            pltpu.VMEM((state, x_cols), jnp.bfloat16),
            pltpu.VMEM((4, state, group), jnp.bfloat16),
            pltpu.VMEM((4, 8, group), jnp.float32),
            pltpu.VMEM((state, group), jnp.bfloat16),
            pltpu.VMEM((8, group), jnp.float32),
            pltpu.VMEM((quads, state, group), jnp.bfloat16),
            pltpu.VMEM((quads, 8, group), jnp.float32),
            pltpu.VMEM((4, state, group), jnp.bfloat16),
            pltpu.VMEM((state, x_cols), jnp.bfloat16),
            dma((4, chunks, 2)),
            dma((4, chunks, 2)),
            dma((2, 4)),
            dma((2, 4)),
            dma((2, quads)),
            dma((2, quads)),
            dma((4,)),
            dma((4,)),
        ],
        compiler_params=pltpu.CompilerParams(
            collective_id=0, has_side_effects=True, vmem_limit_bytes=58 << 20
        ),
        name="attention_and_recurrence",
    )(*args)


def solution(mesh):
    split = P(("groups", "seq"), None)
    return jax.shard_map(
        on_device,
        mesh=mesh,
        in_specs=(split,) * 7 + (P(), P()),
        out_specs=(split, split),
        check_vma=False,
    )
```

time: 591 us -> 202 us (0.34); the launches traced: 584 us -> 201 us
  Pallas kernels: 0 us -> 186 us
  blocking collectives: 138 us -> 0 us
  waiting for transfers between devices: 138 us -> 0 us
  matrix products: 120 us -> 0 us
  local copies, waits for them, and re-layouts: 98.3 us -> 11.2 us
  other arithmetic: 67.1 us -> 2.98 us
  between operations: 15.1 us -> 0.68 us
  starting transfers between devices: 7.69 us -> 0 us
    pallas_call x0 -> x1, Pallas kernels: none -> 186 us  [on_device(): pl.pallas_call(functools.partial(kernel, size), in_specs=[vmem] * len(arg...]
    ppermute x4 -> x0, waiting for transfers between devices: 138 us -> none  [passed_along(): return lax.ppermute(block, axis, route)]
    unnamed x1 -> x0, blocking collectives: 138 us -> none
    dot_general x12 -> x0, matrix products: 64.7 us -> none  [the longest x4 45.7 us: one_group(): jnp.einsum('grk,kge->rge', attn_probs, value_group, preferred_element_typ...]
    sub x4 -> x0, matrix products: 55.1 us -> none  [one_group(): exp_scores = jnp.exp(scores - row_max)]
    dynamic_slice x20 -> x0, local copies, waits for them, and re-layouts: 54.8 us -> none  [the longest x8 35.2 us: one_group(): lax.dynamic_slice_in_dim(keys_all, column, group_cols, 1)]
    select_n x16 -> x0, other arithmetic: 43 us -> none  [hop(): return jax.tree.map(lambda a, b: jnp.where(reached, a, b), new, before)]
    and x4 -> x0, other arithmetic: 14.6 us -> none  [window_attention(): (key_pos[None, :] <= query_pos[:, None]) & (key_pos[None, :] > query_pos[...]
  transfers between devices with their start and end apart: 5 -> 0, of which waited for: 3 -> 0; matrix products, arithmetic and copies ran while one was open for 35% -> 0% of each run, Pallas kernels for 0% -> 0%
where the time goes in v1:
time: 202 us; the launch traced here: 201 us
  Pallas kernels  186 us (92%)
  local copies, waits for them, and re-layouts  11.2 us (6%)
  other arithmetic  2.98 us (1%)
    pallas_call x1, Pallas kernels, on_device(): pl.pallas_call(functools.partial(kernel, size), in_specs=[vmem] * len(arg...  186 us
    unnamed x7, local copies, waits for them, and re-layouts  6.29 us

profile of v1, /device:TPU:8, one launch (start us, length us, event | category | flops | bytes accessed | tf_op | source)
XLA Modules:
  0.0 201.4 jit_solution(9056578299321786631)
XLA Ops:
  0.6 0.7 neg.4
  1.3 0.7 broadcast_in_dim.18
  2.0 0.7 broadcast_in_dim_reshape.3.skip_ref
  2.7 0.9 convert_multiply_fusion
  3.6 1.2 reduce-window.6
  4.8 0.2 slice_reduce_fusion
  5.0 1.7 copy.22
  6.7 0.1 bitcast_bitcast_fusion.1
  6.7 0.2 slice_reduce_fusion.1
  6.9 0.1 broadcast_subtract_fusion
  7.0 0.1 reduce_prod.12
  7.1 0.1 broadcast_in_dim.16
  7.2 0.1 broadcast_in_dim.15
  7.3 0.7 reshape.36.decay_ref
  7.9 0.6 broadcast_in_dim.17.dev_ref
  8.6 0.0 copy-start.1
  8.6 0.8 copy.27
  9.4 0.8 copy.28.cum_ref
  10.2 0.0 copy-done.1
  10.3 186.5 %attention_and_recurrence.1 = (bf16[512,2048]{1,0:T(8,128)(2,1)}, bf16[512,2048]{1,0:T(8,128)(2,1)}) custom-call(bf16[512,2048]{1,0:T(8,128)(2,1)} %q_ref.1, bf16[512,2048]{1,0:T(8,128)(2,1)} %k_ref.1, bf16[512,2048]{1,0:T(8,128)(2,1)} %v_ref.1, bf16[512,2048]{1,0:T(8,128)(2,1)} %x_ref.1, bf16[512,128]{1,0:T(8,128)(2,1)} %b_ref.1, ...), custom_call_target="tpu_custom_call" | custom-call | tf_op jit(solution)/shard_map/attention_and_recurrence/pallas_call | solution.py:395
  196.7 0.0 copy-start
  196.7 3.3 %copy.42 = bf16[512,2048]{1,0:T(8,128)(2,1)} copy(bf16[512,2048]{1,0:T(8,128)(2,1)} %get-tuple-element.8) | data formatting | bytes 4194304
  200.1 0.0 copy-done
  200.1 1.3 copy.43
  (5 shorter events, 0.1 us)
Async XLA Ops:
  8.6 1.7 copy-start.1
  196.7 3.3 %copy-start = (bf16[512,2048]{1,0:T(8,128)(2,1)S(1)}, bf16[512,2048]{1,0:T(8,128)(2,1)}, u32[]{:S(2)}) copy-start(bf16[512,2048]{1,0:T(8,128)(2,1)} %get-tuple-element.9) | copy-start | bytes 6291460

commit v2 on v1

--- a/solution.py
+++ b/solution.py
@@ -12,7 +12,6 @@
 W = 2048
 Q = 256
 CHUNK = 256
-AHEAD = 3
 NEG = -1e30
 LOG2E = math.log2(math.e)
 MESH = pl.DeviceIdType.MESH
@@ -202,15 +201,15 @@
     def offer(chunk):
         send_own(Z, chunk)
 
+        @pl.when(core == 0)
+        def _():
+            send_own(B, chunk)
+
+    def relay(chunk):
         @pl.when(row == 0)
         def _():
             send_own(Y, chunk)
 
-        @pl.when(core == 0)
-        def _():
-            send_own(B, chunk)
-
-    def relay(chunk):
         arrived(Z, chunk)
 
         @pl.when(row == 1)
@@ -221,8 +220,12 @@
         def _():
             pass_on(B, chunk, Z)
 
-    for chunk in range(min(AHEAD, chunks)):
-        offer(chunk)
+    ahead = 2 - core
+    offer(0)
+
+    @pl.when(core == 0)
+    def _():
+        offer(1)
 
     def columns(which):
         return pl.ds(pl.multiple_of(which * group, group), group)
@@ -309,15 +312,16 @@
     }
 
     relay(0)
+    offer(ahead)
 
     def step(j, carry):
-        @pl.when(j + AHEAD < chunks)
-        def _():
-            offer(j + AHEAD)
-
         @pl.when(j + 1 < chunks)
         def _():
             relay(j + 1)
+
+        @pl.when(j + 1 + ahead < chunks)
+        def _():
+            offer(j + 1 + ahead)
 
         @pl.when(j < chunks)
         def _():

time: 202 us -> 189 us (0.936)
  Pallas kernels: 186 us -> 174 us
    pallas_call x1, Pallas kernels: 186 us -> 174 us  [on_device(): pl.pallas_call(functools.partial(kernel, size), in_specs=[vmem] * len(arg...]
where the time goes in v2:
time: 189 us
  Pallas kernels  174 us (92%)
  local copies, waits for them, and re-layouts  11.2 us (6%)
  other arithmetic  2.98 us (2%)
    pallas_call x1, Pallas kernels, on_device(): pl.pallas_call(functools.partial(kernel, size), in_specs=[vmem] * len(arg...  174 us
    unnamed x7, local copies, waits for them, and re-layouts  6.29 us

profile of v2, /device:TPU:8, one launch (start us, length us, event | category | flops | bytes accessed | tf_op | source)
XLA Modules:
  0.0 189.2 jit_solution(11633539060858924735)
XLA Ops:
  0.6 0.7 neg.4
  1.3 0.7 broadcast_in_dim.18
  2.0 0.7 broadcast_in_dim_reshape.3.skip_ref
  2.7 0.9 convert_multiply_fusion
  3.6 1.2 reduce-window.6
  4.8 0.2 slice_reduce_fusion
  5.0 1.7 copy.22
  6.7 0.1 bitcast_bitcast_fusion.1
  6.7 0.2 slice_reduce_fusion.1
  6.9 0.1 broadcast_subtract_fusion
  7.0 0.1 reduce_prod.12
  7.1 0.1 broadcast_in_dim.16
  7.2 0.1 broadcast_in_dim.15
  7.3 0.7 reshape.36.decay_ref
  7.9 0.6 broadcast_in_dim.17.dev_ref
  8.6 0.0 copy-start.1
  8.6 0.8 copy.27
  9.4 0.8 copy.28.cum_ref
  10.2 0.0 copy-done.1
  10.3 174.3 %attention_and_recurrence.1 = (bf16[512,2048]{1,0:T(8,128)(2,1)}, bf16[512,2048]{1,0:T(8,128)(2,1)}) custom-call(bf16[512,2048]{1,0:T(8,128)(2,1)} %q_ref.1, bf16[512,2048]{1,0:T(8,128)(2,1)} %k_ref.1, bf16[512,2048]{1,0:T(8,128)(2,1)} %v_ref.1, bf16[512,2048]{1,0:T(8,128)(2,1)} %x_ref.1, bf16[512,128]{1,0:T(8,128)(2,1)} %b_ref.1, ...), custom_call_target="tpu_custom_call" | custom-call | tf_op jit(solution)/shard_map/attention_and_recurrence/pallas_call | solution.py:399
  184.6 0.0 copy-start
  184.6 3.3 %copy.42 = bf16[512,2048]{1,0:T(8,128)(2,1)} copy(bf16[512,2048]{1,0:T(8,128)(2,1)} %get-tuple-element.8) | data formatting | bytes 4194304
  187.9 0.0 copy-done
  187.9 1.3 copy.43
  (5 shorter events, 0.1 us)
Async XLA Ops:
  8.6 1.7 copy-start.1
  184.6 3.3 %copy-start = (bf16[512,2048]{1,0:T(8,128)(2,1)S(1)}, bf16[512,2048]{1,0:T(8,128)(2,1)}, u32[]{:S(2)}) copy-start(bf16[512,2048]{1,0:T(8,128)(2,1)} %get-tuple-element.9) | copy-start | bytes 6291460
